TPU v7x, 32 devices: a whole 2x2x4 slice. The times are simulated.
32 devices in a mesh: blk: 16 (over z, y, core), tp: 2 (over x).
Axes of the slice: x: 2, y: 2, z: 4, core: 2. Of those that a mesh axis runs over, the one named last changes fastest.
Arguments:
- frames: bfloat16 [4096, 1024], P('blk'), may hold values from -6 to 6
- clip_lengths: int32 [8], replicated, may hold values from 1 to 3841, 4096 in all
- text_states: bfloat16 [128, 1024], replicated, may hold values from -6 to 6
- text_segments: int32 [128], replicated, may hold values from 0 to 7, never falling along the last dimension, each value on 1 to 32 neighbouring positions
- gain_one: float32 [1024], replicated, may hold values from 0.1 to 1.9
- shift_one: float32 [1024], replicated, may hold values from -1.5 to 1.5
- gain_two: float32 [1024], replicated, may hold values from 0.1 to 1.9
- shift_two: float32 [1024], replicated, may hold values from -1.5 to 1.5
- gain_three: float32 [1024], replicated, may hold values from 0.1 to 1.9
- shift_three: float32 [1024], replicated, may hold values from -1.5 to 1.5
- query_weight: bfloat16 [1024, 1024], P(None, 'tp'), may hold values from -0.1875 to 0.1875
- key_weight: bfloat16 [1024, 1024], P(None, 'tp'), may hold values from -0.1875 to 0.1875
- value_weight: bfloat16 [1024, 1024], P(None, 'tp'), may hold values from -0.1875 to 0.1875
- output_weight: bfloat16 [1024, 1024], P('tp'), may hold values from -0.75 to 0.75
- cross_query: bfloat16 [1024, 1024], P(None, 'tp'), may hold values from -0.1875 to 0.1875
- cross_key: bfloat16 [1024, 1024], P(None, 'tp'), may hold values from -0.1875 to 0.1875
- cross_value: bfloat16 [1024, 1024], P(None, 'tp'), may hold values from -0.1875 to 0.1875
- cross_output: bfloat16 [1024, 1024], P('tp'), may hold values from -0.375 to 0.375
- inner_weight: bfloat16 [1024, 4096], P(None, 'tp'), may hold values from -0.1875 to 0.1875
- outer_weight: bfloat16 [4096, 1024], P('tp'), may hold values from -0.09375 to 0.09375
- cotangent: bfloat16 [4096, 1024], P('blk'), may hold values from -6 to 6
Outputs:
- result: bfloat16 [4096, 1024], P('blk')
- grad_frames: bfloat16 [4096, 1024], P('blk')
- grad_text: float32 [128, 1024], replicated
- grad_gain_one: float32 [1024], replicated
- grad_shift_one: float32 [1024], replicated
- grad_gain_two: float32 [1024], replicated
- grad_shift_two: float32 [1024], replicated
- grad_gain_three: float32 [1024], replicated
- grad_shift_three: float32 [1024], replicated
- grad_query_weight: float32 [1024, 1024], P(None, 'tp')
- grad_key_weight: float32 [1024, 1024], P(None, 'tp')
- grad_value_weight: float32 [1024, 1024], P(None, 'tp')
- grad_output_weight: float32 [1024, 1024], P('tp')
- grad_cross_query: float32 [1024, 1024], P(None, 'tp')
- grad_cross_key: float32 [1024, 1024], P(None, 'tp')
- grad_cross_value: float32 [1024, 1024], P(None, 'tp')
- grad_cross_output: float32 [1024, 1024], P('tp')
- grad_inner_weight: float32 [1024, 4096], P(None, 'tp')
- grad_outer_weight: float32 [4096, 1024], P('tp')
Inputs may be any that keep to these rules, and one draw needn't show every extreme that they name: `clip_lengths`: clips follow one another in the pack; one of them has 3841 frames. `text_segments`: text tokens of a clip stand together and in clip order; every clip has 1 to 32 of them, one exactly 32.
All inputs are finite; a program needn't handle non-finite values.
Results may differ from a plain program's by a relative error of at most 0.028.
Values may be sent and summed in bfloat16 or wider, within the bound.
No kernel may reach another device: no remote copies, remote signals or barrier semaphores. Data moves between devices by JAX's collectives and lax.ppermute only.
A program may use at most 384 MiB of HBM per device.

v0:
```python
import jax
import jax.numpy as jnp
from jax import lax
from jax.sharding import PartitionSpec as P

HEAD_DIM = 64
EPSILON = 1e-05
NEGATIVE = -1e30


def shifted(block, axis, distance):
    devices = range(lax.axis_size(axis))
    route = [(i - distance, i) for i in devices if i - distance in devices]
    return lax.ppermute(block, axis, route)


def shifted_2(value, axis, by):
    size = lax.axis_size(axis)
    return lax.ppermute(value, axis, [(i, (i + by) % size) for i in range(size)])


def layer_norm(values, gain, shift):
    centre = values - jnp.mean(values, axis=-1, keepdims=True)
    spread = jnp.mean(centre * centre, axis=-1, keepdims=True)
    return centre * lax.rsqrt(spread + EPSILON) * gain + shift


def norm_grads(values, gain, shift, grad):
    _, pullback = jax.vjp(layer_norm, values, gain, shift)
    return pullback(grad)


def gelu_exact(values):
    return jax.nn.gelu(values, approximate=False)


def clip_rows(positions, clip_lengths):
    ends = jnp.cumsum(clip_lengths)
    starts = ends - clip_lengths
    segment = jnp.sum((positions[:, None] >= ends[None, :]).astype(jnp.int32), axis=1)
    match = segment[:, None] == jnp.arange(clip_lengths.shape[0], dtype=jnp.int32)[None, :]
    first = jnp.sum(jnp.where(match, starts[None, :], 0), axis=1)
    return (segment, first)


def matmul(left, right):
    return jnp.dot(left, right, preferred_element_type=jnp.float32)


def head_sum(values):
    return lax.psum(values.astype(jnp.bfloat16), "tp").astype(jnp.float32)


def unchanged(state):
    return state


def block_grads(
    query_heads,
    grad_heads,
    log_total,
    delta,
    query_rows,
    query_first,
    key_heads,
    value_heads,
    key_rows,
):
    allowed = (key_rows[None, :] <= query_rows[:, None]) & (
        key_rows[None, :] >= query_first[:, None]
    )
    score = jnp.einsum("qhd,khd->hqk", query_heads, key_heads, preferred_element_type=jnp.float32)
    weights = jnp.exp(jnp.where(allowed[None], score - log_total[:, :, None], NEGATIVE))
    grad_weights = jnp.einsum(
        "qhd,khd->hqk", grad_heads, value_heads, preferred_element_type=jnp.float32
    )
    grad_score = (weights * (grad_weights - delta[:, :, None])).astype(jnp.bfloat16)
    query_part = jnp.einsum(
        "hqk,khd->qhd", grad_score, key_heads, preferred_element_type=jnp.float32
    )
    key_part = jnp.einsum(
        "hqk,qhd->khd", grad_score, query_heads, preferred_element_type=jnp.float32
    )
    value_part = jnp.einsum(
        "hqk,qhd->khd", weights.astype(jnp.bfloat16), grad_heads, preferred_element_type=jnp.float32
    )
    return (query_part, key_part, value_part)


def shards(
    frames,
    clip_lengths,
    text_states,
    text_segments,
    gain_one,
    shift_one,
    gain_two,
    shift_two,
    gain_three,
    shift_three,
    query_weight,
    key_weight,
    value_weight,
    output_weight,
    cross_query,
    cross_key,
    cross_value,
    cross_output,
    inner_weight,
    outer_weight,
    cotangent,
):
    row_count = frames.shape[0]
    text_count = text_states.shape[0]
    width_here = query_weight.shape[1]
    heads_here = width_here // HEAD_DIM
    blk_count = lax.axis_size("blk")
    blk_index = lax.axis_index("blk")
    scale = float(HEAD_DIM) ** (-0.5)
    my_first_row = blk_index * row_count
    offsets = jnp.arange(row_count, dtype=jnp.int32)
    rows = my_first_row + offsets
    segment, first = clip_rows(rows, clip_lengths)
    inputs = frames.astype(jnp.float32)
    normed_one = layer_norm(inputs, gain_one, shift_one).astype(jnp.bfloat16)
    queries = (matmul(normed_one, query_weight) * scale).astype(jnp.bfloat16)
    keys = matmul(normed_one, key_weight).astype(jnp.bfloat16)
    values = matmul(normed_one, value_weight).astype(jnp.bfloat16)
    query_heads = queries.reshape(row_count, heads_here, HEAD_DIM)
    start_state = (
        jnp.zeros((row_count, heads_here, HEAD_DIM), jnp.float32),
        jnp.full((heads_here, row_count), NEGATIVE, jnp.float32),
        jnp.zeros((heads_here, row_count), jnp.float32),
    )
    start = jnp.int32(0)
    key_piece = lax.all_gather(keys, "blk", axis=0, tiled=True)
    value_piece = lax.all_gather(values, "blk", axis=0, tiled=True)
    count = key_piece.shape[0]
    key_rows = jnp.arange(count, dtype=jnp.int32)

    def fold_work(state):
        totals, run_max, run_sum = state
        piece_keys = key_piece.reshape(count, heads_here, HEAD_DIM)
        piece_values = value_piece.reshape(count, heads_here, HEAD_DIM)
        score = jnp.einsum(
            "qhd,khd->hqk", query_heads, piece_keys, preferred_element_type=jnp.float32
        )
        allowed = (key_rows[None, :] <= rows[:, None]) & (key_rows[None, :] >= first[:, None])
        masked = jnp.where(allowed[None], score, NEGATIVE)
        new_max = jnp.maximum(run_max, jnp.max(masked, axis=-1))
        expo = jnp.where(allowed[None], jnp.exp(masked - new_max[:, :, None]), 0.0)
        run_sum = jnp.sum(expo, axis=-1)
        added = jnp.einsum(
            "hqk,khd->qhd",
            expo.astype(jnp.bfloat16),
            piece_values,
            preferred_element_type=jnp.float32,
        )
        totals = added
        return (totals, new_max, run_sum)

    needed = (start <= rows[-1]) & (start + count - 1 >= first[0])
    totals, run_max, run_sum = lax.cond(needed, fold_work, unchanged, start_state)
    self_out = totals / jnp.transpose(run_sum)[:, :, None]
    log_total = run_max + jnp.log(run_sum)
    attended = self_out.reshape(row_count, width_here).astype(jnp.bfloat16)
    first_sum = inputs + head_sum(matmul(attended, output_weight))
    normed_two = layer_norm(first_sum, gain_two, shift_two).astype(jnp.bfloat16)
    cross_queries = (matmul(normed_two, cross_query) * scale).astype(jnp.bfloat16)
    text_keys = matmul(text_states, cross_key).astype(jnp.bfloat16)
    text_values = matmul(text_states, cross_value).astype(jnp.bfloat16)
    cross_heads = cross_queries.reshape(row_count, heads_here, HEAD_DIM)
    text_key_heads = text_keys.reshape(text_count, heads_here, HEAD_DIM)
    text_value_heads = text_values.reshape(text_count, heads_here, HEAD_DIM)
    allowed_text = segment[:, None] == text_segments[None, :]
    cross_score = jnp.einsum(
        "qhd,khd->hqk", cross_heads, text_key_heads, preferred_element_type=jnp.float32
    )
    cross_masked = jnp.where(allowed_text[None], cross_score, NEGATIVE)
    cross_max = jnp.max(cross_masked, axis=-1, keepdims=True)
    cross_expo = jnp.where(allowed_text[None], jnp.exp(cross_masked - cross_max), 0.0)
    cross_weights = cross_expo / jnp.sum(cross_expo, axis=-1, keepdims=True)
    cross_weights_low = cross_weights.astype(jnp.bfloat16)
    cross_out = jnp.einsum(
        "hqk,khd->qhd", cross_weights_low, text_value_heads, preferred_element_type=jnp.float32
    )
    crossed = cross_out.reshape(row_count, width_here).astype(jnp.bfloat16)
    second_sum = first_sum + head_sum(matmul(crossed, cross_output))
    normed_three = layer_norm(second_sum, gain_three, shift_three).astype(jnp.bfloat16)
    hidden_pre = matmul(normed_three, inner_weight)
    hidden = gelu_exact(hidden_pre).astype(jnp.bfloat16)
    output = second_sum + head_sum(matmul(hidden, outer_weight))
    grad_output = cotangent.astype(jnp.float32)
    grad_outer = matmul(hidden.T, cotangent)
    grad_hidden = matmul(cotangent, outer_weight.T)
    _, gelu_back = jax.vjp(gelu_exact, hidden_pre)
    grad_pre = gelu_back(grad_hidden)[0].astype(jnp.bfloat16)
    grad_inner = matmul(normed_three.T, grad_pre)
    grad_normed_three = head_sum(matmul(grad_pre, inner_weight.T))
    through_three, grad_gain_three, grad_shift_three = norm_grads(
        second_sum, gain_three, shift_three, grad_normed_three
    )
    grad_second = grad_output + through_three
    grad_second_low = grad_second.astype(jnp.bfloat16)
    grad_cross_output = matmul(crossed.T, grad_second_low)
    grad_crossed = (
        matmul(grad_second_low, cross_output.T)
        .astype(jnp.bfloat16)
        .reshape(row_count, heads_here, HEAD_DIM)
    )
    grad_cross_weights = jnp.einsum(
        "qhd,khd->hqk", grad_crossed, text_value_heads, preferred_element_type=jnp.float32
    )
    cross_delta = jnp.transpose(jnp.sum(grad_crossed.astype(jnp.float32) * cross_out, axis=-1))
    grad_cross_score = (cross_weights * (grad_cross_weights - cross_delta[:, :, None])).astype(
        jnp.bfloat16
    )
    grad_cross_heads = jnp.einsum(
        "hqk,khd->qhd", grad_cross_score, text_key_heads, preferred_element_type=jnp.float32
    ).astype(jnp.bfloat16)
    grad_cross_queries = (grad_cross_heads * scale).reshape(row_count, width_here)
    text_key_part = jnp.einsum(
        "hqk,qhd->khd", grad_cross_score, cross_heads, preferred_element_type=jnp.float32
    )
    text_value_part = jnp.einsum(
        "hqk,qhd->khd", cross_weights_low, grad_crossed, preferred_element_type=jnp.float32
    )
    grad_text_keys, grad_text_values = lax.psum(
        (
            text_key_part.reshape(text_count, width_here),
            text_value_part.reshape(text_count, width_here),
        ),
        "blk",
    )
    grad_text_keys = grad_text_keys.astype(jnp.bfloat16)
    grad_text_values = grad_text_values.astype(jnp.bfloat16)
    grad_cross_key = matmul(text_states.T, grad_text_keys)
    grad_cross_value = matmul(text_states.T, grad_text_values)
    grad_text = lax.psum(
        (matmul(grad_text_keys, cross_key.T) + matmul(grad_text_values, cross_value.T)).astype(
            jnp.bfloat16
        ),
        "tp",
    ).astype(jnp.float32)
    grad_cross_query = matmul(normed_two.T, grad_cross_queries)
    grad_normed_two = head_sum(matmul(grad_cross_queries, cross_query.T))
    through_two, grad_gain_two, grad_shift_two = norm_grads(
        first_sum, gain_two, shift_two, grad_normed_two
    )
    grad_first = grad_second + through_two
    grad_first_low = grad_first.astype(jnp.bfloat16)
    grad_output_weight = matmul(attended.T, grad_first_low)
    grad_attended = matmul(grad_first_low, output_weight.T).astype(jnp.bfloat16)
    grad_heads = grad_attended.reshape(row_count, heads_here, HEAD_DIM)
    self_delta = jnp.transpose(jnp.sum(grad_heads.astype(jnp.float32) * self_out, axis=-1))
    zero_block = jnp.zeros((row_count, width_here), jnp.float32)

    def key_turn(turn, carry):
        source = (blk_index - turn) % blk_count
        base = source * row_count

        def key_work(state):
            key_block, value_block, key_grad, value_grad, query_grad = state
            query_part, key_part, value_part = block_grads(
                query_heads,
                grad_heads,
                log_total,
                self_delta,
                rows,
                first,
                key_block.reshape(row_count, heads_here, HEAD_DIM),
                value_block.reshape(row_count, heads_here, HEAD_DIM),
                base + offsets,
            )
            return (
                key_block,
                value_block,
                key_grad + key_part.reshape(row_count, width_here),
                value_grad + value_part.reshape(row_count, width_here),
                query_grad + query_part.reshape(row_count, width_here),
            )

        needed = (base <= rows[-1]) & (base + row_count - 1 >= first[0])
        key_block, value_block, key_grad, value_grad, query_grad = lax.cond(
            needed, key_work, unchanged, carry
        )
        key_block, value_block = shifted((key_block, value_block), "blk", 1)
        key_grad, value_grad = (
            shifted_2(key_grad.astype(jnp.bfloat16), "blk", 1).astype(key_grad.dtype),
            shifted_2(value_grad.astype(jnp.bfloat16), "blk", 1).astype(value_grad.dtype),
        )
        return (key_block, value_block, key_grad, value_grad, query_grad)

    final = lax.fori_loop(
        0, blk_count, key_turn, (keys, values, zero_block, zero_block, zero_block)
    )
    key_total, value_total, query_total = (final[2], final[3], final[4])
    grad_queries = query_total.astype(jnp.bfloat16) * scale
    grad_keys = key_total.astype(jnp.bfloat16)
    grad_values = value_total.astype(jnp.bfloat16)
    grad_query_weight = matmul(normed_one.T, grad_queries)
    grad_key_weight = matmul(normed_one.T, grad_keys)
    grad_value_weight = matmul(normed_one.T, grad_values)
    grad_normed_one = head_sum(
        matmul(grad_queries, query_weight.T)
        + matmul(grad_keys, key_weight.T)
        + matmul(grad_values, value_weight.T)
    )
    through_one, grad_gain_one, grad_shift_one = norm_grads(
        inputs, gain_one, shift_one, grad_normed_one
    )
    grad_frames = (grad_first + through_one).astype(jnp.bfloat16)
    (
        grad_query_weight,
        grad_key_weight,
        grad_value_weight,
        grad_output_weight,
        grad_cross_query,
        grad_cross_output,
        grad_inner,
        grad_outer,
        grad_gain_one,
        grad_shift_one,
        grad_gain_two,
        grad_shift_two,
        grad_gain_three,
        grad_shift_three,
    ) = lax.psum(
        (
            grad_query_weight,
            grad_key_weight,
            grad_value_weight,
            grad_output_weight,
            grad_cross_query,
            grad_cross_output,
            grad_inner,
            grad_outer,
            grad_gain_one,
            grad_shift_one,
            grad_gain_two,
            grad_shift_two,
            grad_gain_three,
            grad_shift_three,
        ),
        "blk",
    )
    return (
        output.astype(jnp.bfloat16),
        grad_frames,
        grad_text,
        grad_gain_one,
        grad_shift_one,
        grad_gain_two,
        grad_shift_two,
        grad_gain_three,
        grad_shift_three,
        grad_query_weight,
        grad_key_weight,
        grad_value_weight,
        grad_output_weight,
        grad_cross_query,
        grad_cross_key,
        grad_cross_value,
        grad_cross_output,
        grad_inner,
        grad_outer,
    )


def solution(mesh):
    return jax.shard_map(
        shards,
        mesh=mesh,
        in_specs=(
            P("blk", None),
            P(),
            P(),
            P(),
            P(),
            P(),
            P(),
            P(),
            P(),
            P(),
            P(None, "tp"),
            P(None, "tp"),
            P(None, "tp"),
            P("tp", None),
            P(None, "tp"),
            P(None, "tp"),
            P(None, "tp"),
            P("tp", None),
            P(None, "tp"),
            P("tp", None),
            P("blk", None),
        ),
        out_specs=(
            P("blk", None),
            P("blk", None),
            P(),
            P(),
            P(),
            P(),
            P(),
            P(),
            P(),
            P(None, "tp"),
            P(None, "tp"),
            P(None, "tp"),
            P("tp", None),
            P(None, "tp"),
            P(None, "tp"),
            P(None, "tp"),
            P("tp", None),
            P(None, "tp"),
            P("tp", None),
        ),
        check_vma=False,
    )
```

profile of v0, /device:TPU:0, one launch (start us, length us, event | category | flops | bytes accessed | tf_op | source)
XLA Modules:
  0.0 1468.9 jit_solution(12834105977165518617)
XLA Ops:
  21.8 44.2 %all-gather.3.cloned.1.call-done = bf16[4096,512]{1,0:T(8,128)(2,1)} async-done(((bf16[256,512]{1,0:T(8,128)(2,1)}), bf16[4096,512]{1,0:T(8,128)(2,1)}) %all-gather.3.cloned.1.call-update) | async-done | bytes 4194320 | tf_op jit(solution)/shard_map/all_gather | solution.py:136
  66.1 51.8 %all-gather.5.cloned.1.call-done = bf16[4096,512]{1,0:T(8,128)(2,1)} async-done(((bf16[256,512]{1,0:T(8,128)(2,1)}), bf16[4096,512]{1,0:T(8,128)(2,1)}) %all-gather.5.cloned.1.call-update) | async-done | bytes 4194320 | tf_op jit(solution)/shard_map/all_gather | solution.py:137
  117.9 62.9 %conditional.2 = (f32[256,8,64]{0,2,1:T(8,128)S(1)}, f32[8,256]{1,0:T(8,128)}, f32[8,256]{1,0:T(8,128)}, f32[8,256]{1,0:T(8,128)S(1)}) conditional(s32[]{:T(128)} %bitcast.13, () %tuple.55, (s32[4096]{0:T(1024)S(1)}, s32[4096]{0:T(1024)S(1)}, s32[256]{0:T(256)}, s32[256]{0:T(256)}, bf16[4096,512]{1,0:T(8,128)(2,1)}, ...), branch_computations={%region_5.6_spmd, %region_6.9_spmd} | conditional | flops 2234513408 | bytes 130910240 | solution.py:163
  125.8 6.3 copy.80
  132.2 15.7 %select_reduce_fusion = (f32[8,256]{1,0:T(8,128)S(1)}, f32[8,256,4096]{2,1,0:T(8,128)}) fusion(pred[256,4096]{1,0:T(8,128)(4,1)S(1)} %compare_and_fusion, bf16[256,8,64]{0,2,1:T(8,128)(2,1)S(1)} %get-tuple-element.475, bf16[4096,8,64]{0,2,1:T(8,128)(2,1)} %bitcast.126), kind=kOutput, calls=%fused_computation.2 | convolution fusion | flops 1090516992 | bytes 39067648 | tf_op jit(solution)/shard_map/cond/branch_1_fun/qhd,khd->hqk/dot_general | solution.py:145
  148.4 15.5 %fusion.7 = f32[256,8,64]{0,2,1:T(8,128)S(1)} fusion(bf16[4096,8,64]{0,2,1:T(8,128)(2,1)} %bitcast.133, f32[8,256,4096]{2,1,0:T(8,128)} %get-tuple-element.768, f32[8,256]{1,0:T(8,128)} %broadcast_maximum_fusion, pred[256,4096]{1,0:T(8,128)(4,1)S(1)} %compare_and_fusion), kind=kOutput, calls=%fused_computation.8 | convolution fusion | flops 1107296256 | bytes 39329792 | tf_op jit(solution)/shard_map/cond/branch_1_fun/hqk,khd->qhd/dot_general | solution.py:153
  163.9 16.2 %fusion.2 = f32[8,256]{1,0:T(8,128)} fusion(f32[8,256,4096]{2,1,0:T(8,128)} %get-tuple-element.768, f32[8,256]{1,0:T(8,128)} %broadcast_maximum_fusion, pred[256,4096]{1,0:T(8,128)(4,1)S(1)} %compare_and_fusion), kind=kLoop, calls=%fused_computation.3 | loop fusion | flops 33552384 | bytes 34619392 | tf_op jit(solution)/shard_map/cond/branch_1_fun/reduce_sum | solution.py:152
  189.6 21.9 %all-reduce.12.cloned.1.call-done = bf16[256,1024]{1,0:T(8,128)(2,1)} async-done(((bf16[256,1024]{1,0:T(8,128)(2,1)}), bf16[256,1024]{1,0:T(8,128)(2,1)}) %all-reduce.12.cloned.1.call-update) | async-done | bytes 524304 | tf_op jit(solution)/shard_map/psum | solution.py:51
  228.4 25.3 %all-reduce.14.cloned.1.call-done = bf16[256,1024]{1,0:T(8,128)(2,1)} async-done(((bf16[256,1024]{1,0:T(8,128)(2,1)}), bf16[256,1024]{1,0:T(8,128)(2,1)}) %all-reduce.14.cloned.1.call-update) | async-done | bytes 524304 | tf_op jit(solution)/shard_map/psum | solution.py:51
  260.2 6.6 add_convert_fusion
  285.1 15.5 %all-reduce.16.cloned.1.call-done = bf16[256,1024]{1,0:T(8,128)(2,1)} async-done(((bf16[256,1024]{1,0:T(8,128)(2,1)}), bf16[256,1024]{1,0:T(8,128)(2,1)}) %all-reduce.16.cloned.1.call-update) | async-done | bytes 524304 | tf_op jit(solution)/shard_map/psum | solution.py:51
  317.8 25.6 %all-reduce.18.cloned.1.call-done = bf16[256,1024]{1,0:T(8,128)(2,1)} async-done(((bf16[256,1024]{1,0:T(8,128)(2,1)}), bf16[256,1024]{1,0:T(8,128)(2,1)}) %all-reduce.18.cloned.1.call-update) | async-done | bytes 524304 | tf_op jit(solution)/shard_map/psum | solution.py:51
  353.3 421.7 %while.26 = (s32[]{:T(128)}, bf16[256,512]{0,1:T(8,128)(2,1)S(1)}, bf16[256,512]{0,1:T(8,128)(2,1)}, f32[256,512]{0,1:T(8,128)}, f32[256,512]{0,1:T(8,128)}, /*i...) while((s32[]{:T(128)}, bf16[256,512]{0,1:T(8,128)(2,1)S(1)}, ...), condition=%wide.region_29.30_spmd.clone, body=%wide.region_26.29_spmd.clone.sunk | while | flops 341115168 | bytes 37714808 | solution.py:294
  413.3 7.3 collective-permute-start.3
  443.0 7.5 collective-permute-start
  473.5 10.1 collective-permute-start.1
  573.9 7.4 collective-permute-start
  604.4 9.1 collective-permute-start.1
  704.7 7.4 collective-permute-start
  735.2 8.1 collective-permute-start.1
  784.6 31.8 %all-reduce.20.cloned.1.call-done = bf16[256,1024]{1,0:T(8,128)(2,1)} async-done(((bf16[256,1024]{1,0:T(8,128)(2,1)}), bf16[256,1024]{1,0:T(8,128)(2,1)}) %all-reduce.20.cloned.1.call-update) | async-done | bytes 524304 | tf_op jit(solution)/shard_map/psum | solution.py:51
  820.2 67.9 %all-reduce.25 = (bf16[128,512]{0,1:T(8,128)(2,1)S(1)}, bf16[128,512]{0,1:T(8,128)(2,1)}, f32[1024]{0:T(1024)}, f32[1024]{0:T(1024)}, f32[1024]{0:T(1024)}, /*in...) all-reduce(f32[128,512]{0,1:T(8,128)S(1)} %bitcast.142, ...), channel_id=1, replica_groups=mesh['blk'=16,'tp'=2] {'blk'}, use_global_device_ids=true, to_apply=%region_33.34 | all-reduce | flops 137216 | bytes 835584 | tf_op jit(solution)/shard_map/psum | solution.py:228
  909.3 13.6 all-reduce.24.cloned.1.call-done
  926.7 512.8 %all-reduce.22.cloned.1.call-done = (f32[1024,512]{1,0:T(8,128)}, f32[1024,512]{1,0:T(8,128)}, f32[1024,512]{1,0:T(8,128)}, f32[512,1024]{1,0:T(8,128)}, f32[102...) async-done(((f32[1024,512]{1,0:T(8,128)}, f32[1024,512]{1,0:T(8,128)}, f32[1024,512]{1,0:T(8,128)}, f32[512,1024]{1,0:T(8,128)}, ...) | async-done | bytes 29360144 | tf_op jit(solution)/shard_map/psum | solution.py:328
  (720 shorter events, 506.8 us)
Async XLA Ops:
  7.3 58.8 %all-gather.3.cloned.1.call-start = ((), (), s32[]{:S(2)}) async-start(), calls=%async_computation | async-start | bytes 4456448 | tf_op jit(solution)/shard_map/all_gather | solution.py:136
  12.7 105.2 %all-gather.5.cloned.1.call-start = ((), (), s32[]{:S(2)}) async-start(), calls=%async_computation.1 | async-start | bytes 4456448 | tf_op jit(solution)/shard_map/all_gather | solution.py:137
  14.0 197.5 %all-reduce.12.cloned.1.call-start = ((), (), s32[]{:S(2)}) async-start(), calls=%async_computation.2 | async-start | bytes 1048576 | tf_op jit(solution)/shard_map/psum | solution.py:51
  184.3 69.4 %all-reduce.14.cloned.1.call-start = ((), (), s32[]{:S(2)}) async-start(), calls=%async_computation.3 | async-start | bytes 1048576 | tf_op jit(solution)/shard_map/psum | solution.py:51
  224.9 75.7 %all-reduce.16.cloned.1.call-start = ((), (), s32[]{:S(2)}) async-start(), calls=%async_computation.4 | async-start | bytes 1048576 | tf_op jit(solution)/shard_map/psum | solution.py:51
  271.9 71.5 %all-reduce.18.cloned.1.call-start = ((), (), s32[]{:S(2)}) async-start(), calls=%async_computation.5 | async-start | bytes 1048576 | tf_op jit(solution)/shard_map/psum | solution.py:51
  314.6 501.9 %all-reduce.20.cloned.1.call-start = ((), (), s32[]{:S(2)}) async-start(), calls=%async_computation.6 | async-start | bytes 1048576 | tf_op jit(solution)/shard_map/psum | solution.py:51
  410.3 17.5 %collective-permute-start.2 = (bf16[256,512]{0,1:T(8,128)(2,1)S(1)}, bf16[256,512]{0,1:T(8,128)(2,1)}, u32[]{:S(2)}, u32[]{:S(2)}) collective-permute-start(bf16[256,512]{0,1:T(8,128)(2,1)S(1)} %convert_element_type.500), channel_id=1, source_target_pairs={{0,2},{2,4},{4,6},{6,8},{8,10},{10,12},{12,14},{14,16},{16,18},{18... | collective-permute-start | bytes 786440 | tf_op jit(solution)/shard_map/while/body/eval_jaxpr/ppermute | solution.py:19
  438.2 17.5 %collective-permute-start.2 = (bf16[256,512]{0,1:T(8,128)(2,1)S(1)}, bf16[256,512]{0,1:T(8,128)(2,1)}, u32[]{:S(2)}, u32[]{:S(2)}) collective-permute-start(bf16[256,512]{0,1:T(8,128)(2,1)S(1)} %convert_element_type.500), channel_id=1, source_target_pairs={{0,2},{2,4},{4,6},{6,8},{8,10},{10,12},{12,14},{14,16},{16,18},{18... | collective-permute-start | bytes 786440 | tf_op jit(solution)/shard_map/while/body/eval_jaxpr/ppermute | solution.py:19
  440.7 16.8 %collective-permute-start.3 = (bf16[256,512]{0,1:T(8,128)(2,1)}, bf16[256,512]{0,1:T(8,128)(2,1)S(1)}, u32[]{:S(2)}, u32[]{:S(2)}) collective-permute-start(bf16[256,512]{0,1:T(8,128)(2,1)} %convert_element_type.502), channel_id=1, source_target_pairs={{0,2},{2,4},{4,6},{6,8},{8,10},{10,12},{12,14},{14,16},{16,18},{18... | collective-permute-start | bytes 786440 | tf_op jit(solution)/shard_map/while/body/eval_jaxpr/ppermute | solution.py:19
  466.1 17.5 %collective-permute-start.2 = (bf16[256,512]{0,1:T(8,128)(2,1)S(1)}, bf16[256,512]{0,1:T(8,128)(2,1)}, u32[]{:S(2)}, u32[]{:S(2)}) collective-permute-start(bf16[256,512]{0,1:T(8,128)(2,1)S(1)} %convert_element_type.500), channel_id=1, source_target_pairs={{0,2},{2,4},{4,6},{6,8},{8,10},{10,12},{12,14},{14,16},{16,18},{18... | collective-permute-start | bytes 786440 | tf_op jit(solution)/shard_map/while/body/eval_jaxpr/ppermute | solution.py:19
  468.6 16.8 %collective-permute-start.3 = (bf16[256,512]{0,1:T(8,128)(2,1)}, bf16[256,512]{0,1:T(8,128)(2,1)S(1)}, u32[]{:S(2)}, u32[]{:S(2)}) collective-permute-start(bf16[256,512]{0,1:T(8,128)(2,1)} %convert_element_type.502), channel_id=1, source_target_pairs={{0,2},{2,4},{4,6},{6,8},{8,10},{10,12},{12,14},{14,16},{16,18},{18... | collective-permute-start | bytes 786440 | tf_op jit(solution)/shard_map/while/body/eval_jaxpr/ppermute | solution.py:19
  541.2 17.5 %collective-permute-start.2 = (bf16[256,512]{0,1:T(8,128)(2,1)S(1)}, bf16[256,512]{0,1:T(8,128)(2,1)}, u32[]{:S(2)}, u32[]{:S(2)}) collective-permute-start(bf16[256,512]{0,1:T(8,128)(2,1)S(1)} %convert_element_type.500), channel_id=1, source_target_pairs={{0,2},{2,4},{4,6},{6,8},{8,10},{10,12},{12,14},{14,16},{16,18},{18... | collective-permute-start | bytes 786440 | tf_op jit(solution)/shard_map/while/body/eval_jaxpr/ppermute | solution.py:19
  543.6 16.8 %collective-permute-start.3 = (bf16[256,512]{0,1:T(8,128)(2,1)}, bf16[256,512]{0,1:T(8,128)(2,1)S(1)}, u32[]{:S(2)}, u32[]{:S(2)}) collective-permute-start(bf16[256,512]{0,1:T(8,128)(2,1)} %convert_element_type.502), channel_id=1, source_target_pairs={{0,2},{2,4},{4,6},{6,8},{8,10},{10,12},{12,14},{14,16},{16,18},{18... | collective-permute-start | bytes 786440 | tf_op jit(solution)/shard_map/while/body/eval_jaxpr/ppermute | solution.py:19
  569.1 17.4 %collective-permute-start.2 = (bf16[256,512]{0,1:T(8,128)(2,1)S(1)}, bf16[256,512]{0,1:T(8,128)(2,1)}, u32[]{:S(2)}, u32[]{:S(2)}) collective-permute-start(bf16[256,512]{0,1:T(8,128)(2,1)S(1)} %convert_element_type.500), channel_id=1, source_target_pairs={{0,2},{2,4},{4,6},{6,8},{8,10},{10,12},{12,14},{14,16},{16,18},{18... | collective-permute-start | bytes 786440 | tf_op jit(solution)/shard_map/while/body/eval_jaxpr/ppermute | solution.py:19
  571.5 16.8 %collective-permute-start.3 = (bf16[256,512]{0,1:T(8,128)(2,1)}, bf16[256,512]{0,1:T(8,128)(2,1)S(1)}, u32[]{:S(2)}, u32[]{:S(2)}) collective-permute-start(bf16[256,512]{0,1:T(8,128)(2,1)} %convert_element_type.502), channel_id=1, source_target_pairs={{0,2},{2,4},{4,6},{6,8},{8,10},{10,12},{12,14},{14,16},{16,18},{18... | collective-permute-start | bytes 786440 | tf_op jit(solution)/shard_map/while/body/eval_jaxpr/ppermute | solution.py:19
  597.0 16.5 %collective-permute-start.2 = (bf16[256,512]{0,1:T(8,128)(2,1)S(1)}, bf16[256,512]{0,1:T(8,128)(2,1)}, u32[]{:S(2)}, u32[]{:S(2)}) collective-permute-start(bf16[256,512]{0,1:T(8,128)(2,1)S(1)} %convert_element_type.500), channel_id=1, source_target_pairs={{0,2},{2,4},{4,6},{6,8},{8,10},{10,12},{12,14},{14,16},{16,18},{18... | collective-permute-start | bytes 786440 | tf_op jit(solution)/shard_map/while/body/eval_jaxpr/ppermute | solution.py:19
  672.8 16.7 %collective-permute-start.2 = (bf16[256,512]{0,1:T(8,128)(2,1)S(1)}, bf16[256,512]{0,1:T(8,128)(2,1)}, u32[]{:S(2)}, u32[]{:S(2)}) collective-permute-start(bf16[256,512]{0,1:T(8,128)(2,1)S(1)} %convert_element_type.500), channel_id=1, source_target_pairs={{0,2},{2,4},{4,6},{6,8},{8,10},{10,12},{12,14},{14,16},{16,18},{18... | collective-permute-start | bytes 786440 | tf_op jit(solution)/shard_map/while/body/eval_jaxpr/ppermute | solution.py:19
  674.5 16.8 %collective-permute-start.3 = (bf16[256,512]{0,1:T(8,128)(2,1)}, bf16[256,512]{0,1:T(8,128)(2,1)S(1)}, u32[]{:S(2)}, u32[]{:S(2)}) collective-permute-start(bf16[256,512]{0,1:T(8,128)(2,1)} %convert_element_type.502), channel_id=1, source_target_pairs={{0,2},{2,4},{4,6},{6,8},{8,10},{10,12},{12,14},{14,16},{16,18},{18... | collective-permute-start | bytes 786440 | tf_op jit(solution)/shard_map/while/body/eval_jaxpr/ppermute | solution.py:19
  699.9 17.4 %collective-permute-start.2 = (bf16[256,512]{0,1:T(8,128)(2,1)S(1)}, bf16[256,512]{0,1:T(8,128)(2,1)}, u32[]{:S(2)}, u32[]{:S(2)}) collective-permute-start(bf16[256,512]{0,1:T(8,128)(2,1)S(1)} %convert_element_type.500), channel_id=1, source_target_pairs={{0,2},{2,4},{4,6},{6,8},{8,10},{10,12},{12,14},{14,16},{16,18},{18... | collective-permute-start | bytes 786440 | tf_op jit(solution)/shard_map/while/body/eval_jaxpr/ppermute | solution.py:19
  702.4 16.8 %collective-permute-start.3 = (bf16[256,512]{0,1:T(8,128)(2,1)}, bf16[256,512]{0,1:T(8,128)(2,1)S(1)}, u32[]{:S(2)}, u32[]{:S(2)}) collective-permute-start(bf16[256,512]{0,1:T(8,128)(2,1)} %convert_element_type.502), channel_id=1, source_target_pairs={{0,2},{2,4},{4,6},{6,8},{8,10},{10,12},{12,14},{14,16},{16,18},{18... | collective-permute-start | bytes 786440 | tf_op jit(solution)/shard_map/while/body/eval_jaxpr/ppermute | solution.py:19
  754.2 16.6 %collective-permute-start.2 = (bf16[256,512]{0,1:T(8,128)(2,1)S(1)}, bf16[256,512]{0,1:T(8,128)(2,1)}, u32[]{:S(2)}, u32[]{:S(2)}) collective-permute-start(bf16[256,512]{0,1:T(8,128)(2,1)S(1)} %convert_element_type.500), channel_id=1, source_target_pairs={{0,2},{2,4},{4,6},{6,8},{8,10},{10,12},{12,14},{14,16},{16,18},{18... | collective-permute-start | bytes 786440 | tf_op jit(solution)/shard_map/while/body/eval_jaxpr/ppermute | solution.py:19
  779.7 143.2 %all-reduce.24.cloned.1.call-start = ((), (), s32[]{:S(2)}) async-start(), calls=%async_computation.8 | async-start | bytes 1572864 | tf_op jit(solution)/shard_map/psum | solution.py:51
  891.9 547.5 %all-reduce.22.cloned.1.call-start = ((), (), s32[]{:S(2)}) async-start(), calls=%async_computation.7 | async-start | bytes 58720256 | tf_op jit(solution)/shard_map/psum | solution.py:328
  (194 other events, 1868.9 us)
Sparse Core Ops, SparseCore 0:
  12.8 53.2 all-gather.2
  68.8 49.0 all-gather.4
  184.4 27.0 all-reduce.11
  225.1 28.5 all-reduce.13
  272.0 28.5 all-reduce.15
  314.7 28.5 all-reduce.17
  779.8 36.5 all-reduce.19
  892.0 30.8 all-reduce.23
  929.9 509.5 all-reduce.21
where the time goes:
time: 1480 us; the launch traced here: 1470 us
  waiting for transfers between devices  749 us (51%)
  starting transfers between devices  234 us (16%)
  local copies, waits for them, and re-layouts  142 us (10%)
  other arithmetic  127 us (9%)
  matrix products  109 us (7%)
  blocking collectives  67.9 us (5%)
  loops' own time  23.5 us (2%)
  between operations  16.3 us (1%)
    psum x1, waiting for transfers between devices, shards(): lax.psum((grad_query_weight, grad_key_weight, grad_value_weight, grad_out...  513 us
    ppermute x32, starting transfers between devices, shifted(): return lax.ppermute(block, axis, route)  149 us
    psum x6, waiting for transfers between devices, head_sum(): return lax.psum(values.astype(jnp.bfloat16), 'tp').astype(jnp.float32)  134 us
    ppermute x32, starting transfers between devices, shifted_2(): lax.ppermute(value, axis, [(i, (i + by) % size) for i in range(size)])  83.7 us
    psum x1, blocking collectives, shards(): lax.psum((text_key_part.reshape(text_count, width_here), text_value_part....  67.9 us
    dot_general x30, matrix products, matmul(): return jnp.dot(left, right, preferred_element_type=jnp.float32)  67 us
    all_gather x1, waiting for transfers between devices, shards(): value_piece = lax.all_gather(values, 'blk', axis=0, tiled=True)  51.8 us
    all_gather x1, waiting for transfers between devices, shards(): key_piece = lax.all_gather(keys, 'blk', axis=0, tiled=True)  44.2 us
  transfers between devices with their start and end apart: 73, of which 15 were waited for; matrix products, arithmetic and copies ran while one was open for 7% of the time, Pallas kernels for 0%

commit v1 on v0

--- a/solution.py
+++ b/solution.py
@@ -2,10 +2,29 @@
 import jax.numpy as jnp
 from jax import lax
 from jax.sharding import PartitionSpec as P
+from jax.lax import axis_index, axis_size, ppermute
 
 HEAD_DIM = 64
 EPSILON = 1e-05
 NEGATIVE = -1e30
+
+
+def enter_scales_in(frame_in):
+    total_devices = axis_size("blk")
+    g_now = range(total_devices)
+    now = map(lambda j0: (j0, (j0 + 1) % total_devices), g_now)
+    block_list = list(now)
+    fresh = range(total_devices)
+    answer = map(lambda j0: (j0, (j0 - 1) % total_devices), fresh)
+    latest, parts_out = ([frame_in], [frame_in])
+    history = list(answer)
+    for _ in range(total_devices // 2):
+        latest.append(ppermute(latest[-1], axis_name="blk", perm=block_list))
+    for _ in range((total_devices - 1) // 2):
+        parts_out.append(ppermute(parts_out[-1], perm=history, axis_name="blk"))
+    right_arr = jnp.concatenate([*latest[::-1], *parts_out[1:]], axis=0)
+    f_next = axis_index("blk")
+    return jnp.roll(right_arr, (f_next - total_devices // 2) * frame_in.shape[0], axis=0)
 
 
 def shifted(block, axis, distance):
@@ -134,7 +153,7 @@
     )
     start = jnp.int32(0)
     key_piece = lax.all_gather(keys, "blk", axis=0, tiled=True)
-    value_piece = lax.all_gather(values, "blk", axis=0, tiled=True)
+    value_piece = enter_scales_in(values)
     count = key_piece.shape[0]
     key_rows = jnp.arange(count, dtype=jnp.int32)
 

time: 1480 us -> 1470 us (level)
  waiting for transfers between devices: 749 us -> 705 us
  starting transfers between devices: 234 us -> 271 us
    all_gather x1 -> x0, waiting for transfers between devices: 51.8 us -> none  [shards(): value_piece = lax.all_gather(values, 'blk', axis=0, tiled=True)]
    all_gather x1, waiting for transfers between devices: 44.2 us -> 0.01 us  [shards(): key_piece = lax.all_gather(keys, 'blk', axis=0, tiled=True)]
    ppermute x0 -> x15, waiting for transfers between devices: none -> 43.8 us  [the longest x8 37.5 us: enter_scales_in(): latest.append(ppermute(latest[-1], axis_name='blk', perm=block_list))]
    unnamed x198 -> x231, local copies, waits for them, and re-layouts: 39 us -> 72.8 us
    ppermute x0 -> x15, starting transfers between devices: none -> 31.7 us  [the longest x7 31.2 us: enter_scales_in(): parts_out.append(ppermute(parts_out[-1], perm=history, axis_name='blk'))]
    while x128 -> x32, local copies, waits for them, and re-layouts: 39.7 us -> 11.6 us
    slice x32, local copies, waits for them, and re-layouts: 41.3 us -> 17.5 us  [key_turn(): needed = (base <= rows[-1]) & (base + row_count - 1 >= first[0])]
  transfers between devices with their start and end apart: 73 -> 87, of which waited for: 15 -> 30; matrix products, arithmetic and copies ran while one was open for 7% -> 10% of each run, Pallas kernels for 0% -> 0%
where the time goes in v1:
time: 1470 us; the launch traced here: 1460 us
  waiting for transfers between devices  705 us (48%)
  starting transfers between devices  271 us (18%)
  local copies, waits for them, and re-layouts  136 us (9%)
  other arithmetic  125 us (9%)
  matrix products  113 us (8%)
  blocking collectives  67.4 us (5%)
  loops' own time  22.9 us (2%)
  between operations  16.8 us (1%)
    psum x1, waiting for transfers between devices, shards(): lax.psum((grad_query_weight, grad_key_weight, grad_value_weight, grad_out...  513 us
    ppermute x32, starting transfers between devices, shifted(): return lax.ppermute(block, axis, route)  156 us
    psum x6, waiting for transfers between devices, head_sum(): return lax.psum(values.astype(jnp.bfloat16), 'tp').astype(jnp.float32)  131 us
    ppermute x32, starting transfers between devices, shifted_2(): lax.ppermute(value, axis, [(i, (i + by) % size) for i in range(size)])  82.9 us
    unnamed x231, local copies, waits for them, and re-layouts  72.8 us
    dot_general x30, matrix products, matmul(): return jnp.dot(left, right, preferred_element_type=jnp.float32)  70 us
    psum x1, blocking collectives, shards(): lax.psum((text_key_part.reshape(text_count, width_here), text_value_part....  67.4 us
    ppermute x8, waiting for transfers between devices, enter_scales_in(): latest.append(ppermute(latest[-1], axis_name='blk', perm=block_list))  37.5 us
  transfers between devices with their start and end apart: 87, of which 30 were waited for; matrix products, arithmetic and copies ran while one was open for 10% of the time, Pallas kernels for 0%

profile of v1, /device:TPU:0, one launch (start us, length us, event | category | flops | bytes accessed | tf_op | source)
XLA Modules:
  0.0 1457.6 jit_solution(5238895054559706508)
XLA Ops:
  15.1 9.0 collective-permute-done.4
  28.6 9.3 collective-permute-done.5
  134.6 75.3 %conditional.2 = (f32[256,8,64]{0,2,1:T(8,128)S(1)}, f32[8,256]{1,0:T(8,128)}, f32[8,256]{1,0:T(8,128)}, f32[8,256]{1,0:T(8,128)S(1)}) conditional(s32[]{:T(128)} %bitcast.10, () %tuple.66, (s32[4096]{0:T(1024)S(1)}, s32[4096]{0:T(1024)S(1)}, s32[256]{0:T(256)S(1)}, s32[256]{0:T(256)S(1)}, bf16[4096,512]{1,0:T(8,128)(2,1)}, ...), branch_computations={%region_5.6_spmd, %region_6.9_spmd.clone} | conditional | flops 2234513408 | bytes 147687616 | solution.py:182
  135.1 11.9 copy.81
  161.2 15.7 %select_reduce_fusion = (f32[8,256]{1,0:T(8,128)S(1)}, f32[8,256,4096]{2,1,0:T(8,128)}) fusion(pred[256,4096]{1,0:T(8,128)(4,1)S(1)} %compare_and_fusion.1, bf16[256,8,64]{0,2,1:T(8,128)(2,1)S(1)} %get-tuple-element.651, bf16[4096,8,64]{0,2,1:T(8,128)(2,1)} %bitcast.126), kind=kOutput, calls=%fused_computation.15 | convolution fusion | flops 1090516992 | bytes 39067648 | tf_op jit(solution)/shard_map/cond/branch_1_fun/qhd,khd->hqk/dot_general | solution.py:164
  177.4 15.6 %fusion.14 = f32[256,8,64]{0,2,1:T(8,128)S(1)} fusion(bf16[4096,8,64]{0,2,1:T(8,128)(2,1)} %bitcast.131, f32[8,256,4096]{2,1,0:T(8,128)} %get-tuple-element.911, f32[8,256]{1,0:T(8,128)} %broadcast_maximum_fusion, pred[256,4096]{1,0:T(8,128)(4,1)S(1)} %compare_and_fusion.1), kind=kOutput, calls=%fused_computation.21 | convolution fusion | flops 1107296256 | bytes 39329792 | tf_op jit(solution)/shard_map/cond/branch_1_fun/hqk,khd->qhd/dot_general | solution.py:172
  193.0 16.2 %fusion.9 = f32[8,256]{1,0:T(8,128)} fusion(f32[8,256,4096]{2,1,0:T(8,128)} %get-tuple-element.911, f32[8,256]{1,0:T(8,128)} %broadcast_maximum_fusion, pred[256,4096]{1,0:T(8,128)(4,1)S(1)} %compare_and_fusion.1), kind=kLoop, calls=%fused_computation.16 | loop fusion | flops 33552384 | bytes 34619392 | tf_op jit(solution)/shard_map/cond/branch_1_fun/reduce_sum | solution.py:171
  218.1 22.2 %all-reduce.12.cloned.1.call-done = bf16[256,1024]{1,0:T(8,128)(2,1)} async-done(((bf16[256,1024]{1,0:T(8,128)(2,1)}), bf16[256,1024]{1,0:T(8,128)(2,1)}) %all-reduce.12.cloned.1.call-update) | async-done | bytes 524304 | tf_op jit(solution)/shard_map/psum | solution.py:70
  254.7 25.3 %all-reduce.14.cloned.1.call-done = bf16[256,1024]{1,0:T(8,128)(2,1)} async-done(((bf16[256,1024]{1,0:T(8,128)(2,1)}), bf16[256,1024]{1,0:T(8,128)(2,1)}) %all-reduce.14.cloned.1.call-update) | async-done | bytes 524304 | tf_op jit(solution)/shard_map/psum | solution.py:70
  311.5 15.5 %all-reduce.16.cloned.1.call-done = bf16[256,1024]{1,0:T(8,128)(2,1)} async-done(((bf16[256,1024]{1,0:T(8,128)(2,1)}), bf16[256,1024]{1,0:T(8,128)(2,1)}) %all-reduce.16.cloned.1.call-update) | async-done | bytes 524304 | tf_op jit(solution)/shard_map/psum | solution.py:70
  345.0 24.9 %all-reduce.18.cloned.1.call-done = bf16[256,1024]{1,0:T(8,128)(2,1)} async-done(((bf16[256,1024]{1,0:T(8,128)(2,1)}), bf16[256,1024]{1,0:T(8,128)(2,1)}) %all-reduce.18.cloned.1.call-update) | async-done | bytes 524304 | tf_op jit(solution)/shard_map/psum | solution.py:70
  381.5 386.0 %while.26 = (s32[]{:T(128)}, bf16[256,512]{0,1:T(8,128)(2,1)S(1)}, bf16[256,512]{0,1:T(8,128)(2,1)S(1)}, f32[256,512]{0,1:T(8,128)}, f32[256,512]{0,1:T(8,128)},...) while((s32[]{:T(128)}, bf16[256,512]{0,1:T(8,128)(2,1)S(1)}, ...), condition=%wide.region_29.30_spmd.clone, body=%wide.region_26.29_spmd.clone.sunk | while | flops 341115168 | bytes 32471788 | solution.py:313
  434.4 8.4 collective-permute-start.3
  462.0 8.6 collective-permute-start
  490.2 11.2 collective-permute-start.1
  552.5 7.4 collective-permute-start.3
  580.6 8.5 collective-permute-start
  608.8 10.2 collective-permute-start.1
  699.2 8.5 collective-permute-start
  727.4 9.2 collective-permute-start.1
  776.7 29.7 %all-reduce.20.cloned.1.call-done = bf16[256,1024]{1,0:T(8,128)(2,1)} async-done(((bf16[256,1024]{1,0:T(8,128)(2,1)}), bf16[256,1024]{1,0:T(8,128)(2,1)}) %all-reduce.20.cloned.1.call-update) | async-done | bytes 524304 | tf_op jit(solution)/shard_map/psum | solution.py:70
  810.0 67.4 %all-reduce.25 = (bf16[128,512]{0,1:T(8,128)(2,1)S(1)}, bf16[128,512]{0,1:T(8,128)(2,1)S(1)}, f32[1024]{0:T(1024)}, f32[1024]{0:T(1024)}, f32[1024]{0:T(1024)}, ...) all-reduce(f32[128,512]{0,1:T(8,128)S(1)} %bitcast.140, ...), channel_id=1, replica_groups=mesh['blk'=16,'tp'=2] {'blk'}, use_global_device_ids=true, to_apply=%region_33.34 | all-reduce | flops 137216 | bytes 835584 | tf_op jit(solution)/shard_map/psum | solution.py:247
  899.0 13.6 all-reduce.24.cloned.1.call-done
  916.4 512.8 %all-reduce.22.cloned.1.call-done = (f32[1024,512]{1,0:T(8,128)}, f32[1024,512]{1,0:T(8,128)}, f32[1024,512]{1,0:T(8,128)}, f32[512,1024]{1,0:T(8,128)}, f32[102...) async-done(((f32[1024,512]{1,0:T(8,128)}, f32[1024,512]{1,0:T(8,128)}, f32[1024,512]{1,0:T(8,128)}, f32[512,1024]{1,0:T(8,128)}, ...) | async-done | bytes 29360144 | tf_op jit(solution)/shard_map/psum | solution.py:347
  (682 shorter events, 563.4 us)
Async XLA Ops:
  7.3 127.3 %all-gather.2.cloned.1.call-start = ((), (), s32[]{:S(2)}) async-start(), calls=%async_computation | async-start | bytes 4456448 | tf_op jit(solution)/shard_map/all_gather | solution.py:155
  12.6 227.6 %all-reduce.12.cloned.1.call-start = ((), (), s32[]{:S(2)}) async-start(), calls=%async_computation.1 | async-start | bytes 1048576 | tf_op jit(solution)/shard_map/psum | solution.py:70
  92.0 23.7 %collective-permute-start.18 = (bf16[256,512]{1,0:T(8,128)(2,1)}, bf16[256,512]{1,0:T(8,128)(2,1)S(1)}, u32[]{:S(2)}, u32[]{:S(2)}) collective-permute-start(bf16[256,512]{1,0:T(8,128)(2,1)} %collective-permute-done.17), channel_id=1, source_target_pairs={{0,30},{2,0},{4,2},{6,4},{8,6},{10,8},{12,10},{14,12},{16,14},{18,... | collective-permute-start | bytes 786440 | tf_op jit(solution)/shard_map/ppermute | solution.py:24
  213.5 66.5 %all-reduce.14.cloned.1.call-start = ((), (), s32[]{:S(2)}) async-start(), calls=%async_computation.2 | async-start | bytes 1048576 | tf_op jit(solution)/shard_map/psum | solution.py:70
  251.3 75.8 %all-reduce.16.cloned.1.call-start = ((), (), s32[]{:S(2)}) async-start(), calls=%async_computation.3 | async-start | bytes 1048576 | tf_op jit(solution)/shard_map/psum | solution.py:70
  298.3 71.6 %all-reduce.18.cloned.1.call-start = ((), (), s32[]{:S(2)}) async-start(), calls=%async_computation.4 | async-start | bytes 1048576 | tf_op jit(solution)/shard_map/psum | solution.py:70
  341.1 465.2 %all-reduce.20.cloned.1.call-start = ((), (), s32[]{:S(2)}) async-start(), calls=%async_computation.5 | async-start | bytes 1048576 | tf_op jit(solution)/shard_map/psum | solution.py:70
  431.5 18.6 %collective-permute-start.2 = (bf16[256,512]{0,1:T(8,128)(2,1)S(1)}, bf16[256,512]{0,1:T(8,128)(2,1)}, u32[]{:S(2)}, u32[]{:S(2)}) collective-permute-start(bf16[256,512]{0,1:T(8,128)(2,1)S(1)} %convert_element_type.504), channel_id=1, source_target_pairs={{0,2},{2,4},{4,6},{6,8},{8,10},{10,12},{12,14},{14,16},{16,18},{18... | collective-permute-start | bytes 786440 | tf_op jit(solution)/shard_map/while/body/eval_jaxpr/ppermute | solution.py:38
  457.1 18.6 %collective-permute-start.2 = (bf16[256,512]{0,1:T(8,128)(2,1)S(1)}, bf16[256,512]{0,1:T(8,128)(2,1)}, u32[]{:S(2)}, u32[]{:S(2)}) collective-permute-start(bf16[256,512]{0,1:T(8,128)(2,1)S(1)} %convert_element_type.504), channel_id=1, source_target_pairs={{0,2},{2,4},{4,6},{6,8},{8,10},{10,12},{12,14},{14,16},{16,18},{18... | collective-permute-start | bytes 786440 | tf_op jit(solution)/shard_map/while/body/eval_jaxpr/ppermute | solution.py:38
  459.6 17.9 %collective-permute-start.3 = (bf16[256,512]{0,1:T(8,128)(2,1)}, bf16[256,512]{0,1:T(8,128)(2,1)S(1)}, u32[]{:S(2)}, u32[]{:S(2)}) collective-permute-start(bf16[256,512]{0,1:T(8,128)(2,1)} %convert_element_type.506), channel_id=1, source_target_pairs={{0,2},{2,4},{4,6},{6,8},{8,10},{10,12},{12,14},{14,16},{16,18},{18... | collective-permute-start | bytes 786440 | tf_op jit(solution)/shard_map/while/body/eval_jaxpr/ppermute | solution.py:38
  482.8 18.6 %collective-permute-start.2 = (bf16[256,512]{0,1:T(8,128)(2,1)S(1)}, bf16[256,512]{0,1:T(8,128)(2,1)}, u32[]{:S(2)}, u32[]{:S(2)}) collective-permute-start(bf16[256,512]{0,1:T(8,128)(2,1)S(1)} %convert_element_type.504), channel_id=1, source_target_pairs={{0,2},{2,4},{4,6},{6,8},{8,10},{10,12},{12,14},{14,16},{16,18},{18... | collective-permute-start | bytes 786440 | tf_op jit(solution)/shard_map/while/body/eval_jaxpr/ppermute | solution.py:38
  485.3 17.9 %collective-permute-start.3 = (bf16[256,512]{0,1:T(8,128)(2,1)}, bf16[256,512]{0,1:T(8,128)(2,1)S(1)}, u32[]{:S(2)}, u32[]{:S(2)}) collective-permute-start(bf16[256,512]{0,1:T(8,128)(2,1)} %convert_element_type.506), channel_id=1, source_target_pairs={{0,2},{2,4},{4,6},{6,8},{8,10},{10,12},{12,14},{14,16},{16,18},{18... | collective-permute-start | bytes 786440 | tf_op jit(solution)/shard_map/while/body/eval_jaxpr/ppermute | solution.py:38
  550.1 18.6 %collective-permute-start.2 = (bf16[256,512]{0,1:T(8,128)(2,1)S(1)}, bf16[256,512]{0,1:T(8,128)(2,1)}, u32[]{:S(2)}, u32[]{:S(2)}) collective-permute-start(bf16[256,512]{0,1:T(8,128)(2,1)S(1)} %convert_element_type.504), channel_id=1, source_target_pairs={{0,2},{2,4},{4,6},{6,8},{8,10},{10,12},{12,14},{14,16},{16,18},{18... | collective-permute-start | bytes 786440 | tf_op jit(solution)/shard_map/while/body/eval_jaxpr/ppermute | solution.py:38
  552.5 17.9 %collective-permute-start.3 = (bf16[256,512]{0,1:T(8,128)(2,1)}, bf16[256,512]{0,1:T(8,128)(2,1)S(1)}, u32[]{:S(2)}, u32[]{:S(2)}) collective-permute-start(bf16[256,512]{0,1:T(8,128)(2,1)} %convert_element_type.506), channel_id=1, source_target_pairs={{0,2},{2,4},{4,6},{6,8},{8,10},{10,12},{12,14},{14,16},{16,18},{18... | collective-permute-start | bytes 786440 | tf_op jit(solution)/shard_map/while/body/eval_jaxpr/ppermute | solution.py:38
  575.8 18.5 %collective-permute-start.2 = (bf16[256,512]{0,1:T(8,128)(2,1)S(1)}, bf16[256,512]{0,1:T(8,128)(2,1)}, u32[]{:S(2)}, u32[]{:S(2)}) collective-permute-start(bf16[256,512]{0,1:T(8,128)(2,1)S(1)} %convert_element_type.504), channel_id=1, source_target_pairs={{0,2},{2,4},{4,6},{6,8},{8,10},{10,12},{12,14},{14,16},{16,18},{18... | collective-permute-start | bytes 786440 | tf_op jit(solution)/shard_map/while/body/eval_jaxpr/ppermute | solution.py:38
  578.2 17.9 %collective-permute-start.3 = (bf16[256,512]{0,1:T(8,128)(2,1)}, bf16[256,512]{0,1:T(8,128)(2,1)S(1)}, u32[]{:S(2)}, u32[]{:S(2)}) collective-permute-start(bf16[256,512]{0,1:T(8,128)(2,1)} %convert_element_type.506), channel_id=1, source_target_pairs={{0,2},{2,4},{4,6},{6,8},{8,10},{10,12},{12,14},{14,16},{16,18},{18... | collective-permute-start | bytes 786440 | tf_op jit(solution)/shard_map/while/body/eval_jaxpr/ppermute | solution.py:38
  601.4 17.6 %collective-permute-start.2 = (bf16[256,512]{0,1:T(8,128)(2,1)S(1)}, bf16[256,512]{0,1:T(8,128)(2,1)}, u32[]{:S(2)}, u32[]{:S(2)}) collective-permute-start(bf16[256,512]{0,1:T(8,128)(2,1)S(1)} %convert_element_type.504), channel_id=1, source_target_pairs={{0,2},{2,4},{4,6},{6,8},{8,10},{10,12},{12,14},{14,16},{16,18},{18... | collective-permute-start | bytes 786440 | tf_op jit(solution)/shard_map/while/body/eval_jaxpr/ppermute | solution.py:38
  672.3 18.6 %collective-permute-start.3 = (bf16[256,512]{0,1:T(8,128)(2,1)}, bf16[256,512]{0,1:T(8,128)(2,1)S(1)}, u32[]{:S(2)}, u32[]{:S(2)}) collective-permute-start(bf16[256,512]{0,1:T(8,128)(2,1)} %convert_element_type.506), channel_id=1, source_target_pairs={{0,2},{2,4},{4,6},{6,8},{8,10},{10,12},{12,14},{14,16},{16,18},{18... | collective-permute-start | bytes 786440 | tf_op jit(solution)/shard_map/while/body/eval_jaxpr/ppermute | solution.py:38
  697.1 18.6 %collective-permute-start.3 = (bf16[256,512]{0,1:T(8,128)(2,1)}, bf16[256,512]{0,1:T(8,128)(2,1)S(1)}, u32[]{:S(2)}, u32[]{:S(2)}) collective-permute-start(bf16[256,512]{0,1:T(8,128)(2,1)} %convert_element_type.506), channel_id=1, source_target_pairs={{0,2},{2,4},{4,6},{6,8},{8,10},{10,12},{12,14},{14,16},{16,18},{18... | collective-permute-start | bytes 786440 | tf_op jit(solution)/shard_map/while/body/eval_jaxpr/ppermute | solution.py:38
  722.4 18.6 %collective-permute-start.3 = (bf16[256,512]{0,1:T(8,128)(2,1)}, bf16[256,512]{0,1:T(8,128)(2,1)S(1)}, u32[]{:S(2)}, u32[]{:S(2)}) collective-permute-start(bf16[256,512]{0,1:T(8,128)(2,1)} %convert_element_type.506), channel_id=1, source_target_pairs={{0,2},{2,4},{4,6},{6,8},{8,10},{10,12},{12,14},{14,16},{16,18},{18... | collective-permute-start | bytes 786440 | tf_op jit(solution)/shard_map/while/body/eval_jaxpr/ppermute | solution.py:38
  746.3 17.6 %collective-permute-start.2 = (bf16[256,512]{0,1:T(8,128)(2,1)S(1)}, bf16[256,512]{0,1:T(8,128)(2,1)}, u32[]{:S(2)}, u32[]{:S(2)}) collective-permute-start(bf16[256,512]{0,1:T(8,128)(2,1)S(1)} %convert_element_type.504), channel_id=1, source_target_pairs={{0,2},{2,4},{4,6},{6,8},{8,10},{10,12},{12,14},{14,16},{16,18},{18... | collective-permute-start | bytes 786440 | tf_op jit(solution)/shard_map/while/body/eval_jaxpr/ppermute | solution.py:38
  748.1 18.6 %collective-permute-start.3 = (bf16[256,512]{0,1:T(8,128)(2,1)}, bf16[256,512]{0,1:T(8,128)(2,1)S(1)}, u32[]{:S(2)}, u32[]{:S(2)}) collective-permute-start(bf16[256,512]{0,1:T(8,128)(2,1)} %convert_element_type.506), channel_id=1, source_target_pairs={{0,2},{2,4},{4,6},{6,8},{8,10},{10,12},{12,14},{14,16},{16,18},{18... | collective-permute-start | bytes 786440 | tf_op jit(solution)/shard_map/while/body/eval_jaxpr/ppermute | solution.py:38
  772.9 139.7 %all-reduce.24.cloned.1.call-start = ((), (), s32[]{:S(2)}) async-start(), calls=%async_computation.7 | async-start | bytes 1572864 | tf_op jit(solution)/shard_map/psum | solution.py:70
  881.6 547.5 %all-reduce.22.cloned.1.call-start = ((), (), s32[]{:S(2)}) async-start(), calls=%async_computation.6 | async-start | bytes 58720256 | tf_op jit(solution)/shard_map/psum | solution.py:347
  (159 other events, 2610.3 us)
Sparse Core Ops, SparseCore 0:
  12.7 67.3 all-gather.1
  213.7 26.5 all-reduce.11
  251.4 28.5 all-reduce.13
  298.4 28.5 all-reduce.15
  341.3 28.5 all-reduce.17
  773.0 33.2 all-reduce.19
  881.7 30.8 all-reduce.23
  919.6 509.5 all-reduce.21
